TPU v7x, 32 devices: a whole 2x2x4 slice. The times are simulated.
32 devices in a mesh: wide: 8 (over y, x, core), tp: 4 (over z).
Axes of the slice: x: 2, y: 2, z: 4, core: 2. Of those that a mesh axis runs over, the one named last changes fastest.
Arguments:
- hidden_in: bfloat16 [8, 1024, 1024], P('tp', 'wide'), may hold values from -6 to 6
- lengths: int32 [8], replicated, may hold values from 256 to 1024, as said below
- pre_gain: bfloat16 [1024], P('wide'), may hold values from 0.5 to 1.5
- pre_shift: bfloat16 [1024], P('wide'), may hold values from -1.796875 to 1.796875
- w_query: bfloat16 [1024, 1024], P('wide', 'tp'), may hold values from -0.1875 to 0.1875
- w_key: bfloat16 [1024, 1024], P('wide', 'tp'), may hold values from -0.1875 to 0.1875
- w_value: bfloat16 [1024, 1024], P('wide', 'tp'), may hold values from -0.1875 to 0.1875
- b_query: bfloat16 [16, 64], P('tp', 'wide'), may hold values from -1.796875 to 1.796875
- b_value: bfloat16 [16, 64], P('tp', 'wide'), may hold values from -1.796875 to 1.796875
- w_dense: bfloat16 [1024, 1024], P('tp', 'wide'), may hold values from -0.75 to 0.75
- b_dense: bfloat16 [1024], P('wide'), may hold values from -1.796875 to 1.796875
- mid_gain: bfloat16 [1024], P('wide'), may hold values from 0.5 to 1.5
- mid_shift: bfloat16 [1024], P('wide'), may hold values from -1.796875 to 1.796875
- w_up: bfloat16 [1024, 4096], P('wide', 'tp'), may hold values from -0.1875 to 0.1875
- b_up: bfloat16 [16, 256], P('tp', 'wide'), may hold values from -1.796875 to 1.796875
- w_down: bfloat16 [4096, 1024], P('tp', 'wide'), may hold values from -0.09375 to 0.09375
- b_down: bfloat16 [1024], P('wide'), may hold values from -1.796875 to 1.796875
- cotangent: bfloat16 [8, 1024, 1024], P('tp', 'wide'), may hold values from -6 to 6
Outputs:
- output: bfloat16 [8, 1024, 1024], P('tp', 'wide')
- grad_in: bfloat16 [8, 1024, 1024], P('tp', 'wide')
- grad_pre_gain: float32 [1024], P('wide')
- grad_pre_shift: float32 [1024], P('wide')
- grad_w_query: float32 [1024, 1024], P('wide', 'tp')
- grad_w_key: float32 [1024, 1024], P('wide', 'tp')
- grad_w_value: float32 [1024, 1024], P('wide', 'tp')
- grad_b_query: float32 [16, 64], P('tp', 'wide')
- grad_b_value: float32 [16, 64], P('tp', 'wide')
- grad_w_dense: float32 [1024, 1024], P('tp', 'wide')
- grad_b_dense: float32 [1024], P('wide')
- grad_mid_gain: float32 [1024], P('wide')
- grad_mid_shift: float32 [1024], P('wide')
- grad_w_up: float32 [1024, 4096], P('wide', 'tp')
- grad_b_up: float32 [16, 256], P('tp', 'wide')
- grad_w_down: float32 [4096, 1024], P('tp', 'wide')
- grad_b_down: float32 [1024], P('wide')
Inputs may be any that keep to these rules, and one draw needn't show every extreme that they name: lengths[s] tokens fill the leading positions of slot s; some slot is full and some holds exactly 256 tokens.
All inputs are finite; a program needn't handle non-finite values.
Results may differ from a plain program's by a relative error of at most 0.02.
Values may be sent and summed in bfloat16 or wider, within the bound.
A program may use at most 192 MiB of HBM per device.

v0:
```python
import math
import jax
import jax.numpy as jnp
from jax import lax
from jax.sharding import PartitionSpec as P

HEAD = 64


def norm_rows(values, gain_vec, shift_vec):
    middle = jnp.mean(values, axis=-1, keepdims=True)
    centred = values - middle
    spread = jnp.mean(centred * centred, axis=-1, keepdims=True)
    return centred * lax.rsqrt(spread + 1e-05) * gain_vec + shift_vec


def flatten_rows(tensor):
    return tensor.reshape(-1, tensor.shape[-1])


def row_product(first_op, second_op):
    return jnp.dot(first_op, second_op, preferred_element_type=jnp.float32)


def inner_rows(first_op, second_op):
    return lax.dot_general(
        flatten_rows(first_op),
        flatten_rows(second_op),
        (((0,), (0,)), ((), ())),
        preferred_element_type=jnp.float32,
    )


def times_transposed(first_op, second_op):
    return lax.dot_general(
        first_op,
        second_op,
        (((first_op.ndim - 1,), (1,)), ((), ())),
        preferred_element_type=jnp.float32,
    )


def activate(values):
    return jax.nn.gelu(values, approximate=True)


def masked_scores(query_blk, key_blk, lengths_blk, slopes, distance, causal_mask, key_places):
    raw_scores = (
        jnp.einsum("gihd,gjhd->ghij", query_blk, key_blk, preferred_element_type=jnp.float32)
        * 0.125
    )
    raw_scores = raw_scores - slopes[None, :, None, None] * distance[None, None]
    allowed = causal_mask[None] & (key_places[None, None, :] < lengths_blk[:, None, None])
    return jnp.where(allowed[:, None], raw_scores, -jnp.inf)


def per_device(
    hidden_in,
    lengths,
    pre_gain,
    pre_shift,
    w_query,
    w_key,
    w_value,
    b_query,
    b_value,
    w_dense,
    b_dense,
    mid_gain,
    mid_shift,
    w_up,
    b_up,
    w_down,
    b_down,
    cotangent,
):
    local_slots, block_len, _unused = hidden_in.shape
    heads_dev = b_query.shape[0]
    head_width = heads_dev * HEAD
    slot_total = local_slots * lax.axis_size("tp")
    slot_len = block_len * lax.axis_size("wide")
    wide_at = lax.axis_index("wide")
    tp_at = lax.axis_index("tp")
    vec_part = pre_gain.shape[0]
    (
        gain_one,
        shift_one,
        query_w,
        key_w,
        value_w,
        query_b,
        value_b,
        dense_w,
        dense_b,
        gain_two,
        shift_two,
        up_w,
        up_b,
        down_w,
        down_b,
    ) = (
        lax.all_gather(pre_gain, "wide", axis=0, tiled=True),
        lax.all_gather(pre_shift, "wide", axis=0, tiled=True),
        lax.all_gather(w_query, "wide", axis=0, tiled=True),
        lax.all_gather(w_key, "wide", axis=0, tiled=True),
        lax.all_gather(w_value, "wide", axis=0, tiled=True),
        lax.all_gather(b_query, "wide", axis=1, tiled=True),
        lax.all_gather(b_value, "wide", axis=1, tiled=True),
        lax.all_gather(w_dense, "wide", axis=1, tiled=True),
        lax.all_gather(b_dense, "wide", axis=0, tiled=True),
        lax.all_gather(mid_gain, "wide", axis=0, tiled=True),
        lax.all_gather(mid_shift, "wide", axis=0, tiled=True),
        lax.all_gather(w_up, "wide", axis=0, tiled=True),
        lax.all_gather(b_up, "wide", axis=1, tiled=True),
        lax.all_gather(w_down, "wide", axis=1, tiled=True),
        lax.all_gather(b_down, "wide", axis=0, tiled=True),
    )
    gain_one = gain_one.astype(jnp.float32)
    shift_one = shift_one.astype(jnp.float32)
    gain_two = gain_two.astype(jnp.float32)
    shift_two = shift_two.astype(jnp.float32)
    query_places = wide_at * block_len + jnp.arange(block_len, dtype=jnp.int32)
    key_places = jnp.arange(slot_len, dtype=jnp.int32)
    distance = (query_places[:, None] - key_places[None, :]).astype(jnp.float32)
    causal_mask = key_places[None, :] <= query_places[:, None]
    head_index = tp_at * heads_dev + jnp.arange(heads_dev, dtype=jnp.int32)
    slopes = jnp.exp2(-0.5 * (head_index.astype(jnp.float32) + 1.0))
    own_lengths = lax.dynamic_slice_in_dim(lengths, tp_at * local_slots, local_slots, 0)
    validity = (query_places[None, :] < own_lengths[:, None]).astype(jnp.float32)
    group_size = math.gcd(slot_total, max(1, 512 // block_len))
    group_count = slot_total // group_size
    grouped_lengths = lengths.reshape(group_count, group_size)
    hidden = hidden_in.astype(jnp.float32)

    def query_view(tensor):
        return tensor.reshape(group_count, group_size, block_len, heads_dev, HEAD)

    def pair_view(tensor):
        return tensor.reshape(group_count, group_size, slot_len, 2, heads_dev, HEAD)

    def forward_group(inputs):
        query_blk, pair_blk, lengths_blk = inputs
        masked = masked_scores(
            query_blk, pair_blk[:, :, 0], lengths_blk, slopes, distance, causal_mask, key_places
        )
        highest = jnp.max(masked, axis=-1, keepdims=True)
        totals = highest + jnp.log(jnp.sum(jnp.exp(masked - highest), axis=-1, keepdims=True))
        probabilities = jnp.exp(masked - totals).astype(jnp.bfloat16)
        summed = jnp.einsum(
            "ghij,gjhd->gihd", probabilities, pair_blk[:, :, 1], preferred_element_type=jnp.float32
        )
        return (totals[..., 0], summed)

    def attention_forward(hidden_rows):
        normed_f, norm_back = jax.vjp(norm_rows, hidden_rows, gain_one, shift_one)
        normed = normed_f.astype(jnp.bfloat16)
        normed_all = lax.all_gather(normed, "tp", axis=0, tiled=True)
        queries = (
            row_product(normed_all, query_w) + query_b.reshape(head_width).astype(jnp.float32)
        ).astype(jnp.bfloat16)
        keys_now = row_product(normed_all, key_w).astype(jnp.bfloat16)
        values_now = (
            row_product(normed_all, value_w) + value_b.reshape(head_width).astype(jnp.float32)
        ).astype(jnp.bfloat16)
        pairs = jnp.concatenate([keys_now, values_now], axis=-1)
        pairs_all = lax.all_gather(pairs, "wide", axis=1, tiled=True)
        totals, summed = lax.map(
            forward_group, (query_view(queries), pair_view(pairs_all), grouped_lengths)
        )
        return (
            normed_all,
            queries,
            pairs_all,
            totals,
            summed.reshape(slot_total, block_len, head_width),
            norm_back,
        )

    forward_parts = attention_forward(hidden)
    attention = forward_parts[4].astype(jnp.bfloat16)
    branch = lax.psum_scatter(
        row_product(attention, dense_w).astype(jnp.bfloat16), "tp", scatter_dimension=0, tiled=True
    ).astype(jnp.float32)
    residual = hidden + branch + dense_b.astype(jnp.float32)
    second_f, second_back = jax.vjp(norm_rows, residual, gain_two, shift_two)
    second = second_f.astype(jnp.bfloat16)
    grad_output = validity[:, :, None] * cotangent.astype(jnp.float32)
    grad_down = grad_output.astype(jnp.bfloat16)
    second_all, grad_down_all = (
        lax.all_gather(second, "tp", axis=0, tiled=True),
        lax.all_gather(grad_down, "tp", axis=0, tiled=True),
    )
    pre_act = row_product(second_all, up_w) + up_b.reshape(-1).astype(jnp.float32)
    act_value, act_back = jax.vjp(activate, pre_act)
    activated = act_value.astype(jnp.bfloat16)
    down_out = lax.psum_scatter(
        row_product(activated, down_w).astype(jnp.bfloat16), "tp", scatter_dimension=0, tiled=True
    ).astype(jnp.float32)
    grad_act = times_transposed(grad_down_all, down_w)
    grad_pre = act_back(grad_act)[0].astype(jnp.bfloat16)
    grad_up = inner_rows(second_all, grad_pre)
    grad_up_b = jnp.sum(flatten_rows(grad_pre), axis=0, dtype=jnp.float32).reshape(up_b.shape)
    grad_down_w = inner_rows(activated, grad_down_all)
    grad_second = lax.psum_scatter(
        times_transposed(grad_pre, up_w), "tp", scatter_dimension=0, tiled=True
    )
    output = (validity[:, :, None] * (residual + down_out + down_b.astype(jnp.float32))).astype(
        jnp.bfloat16
    )
    grad_resid_norm, grad_gain_two, grad_shift_two = second_back(grad_second)
    grad_resid = grad_output + grad_resid_norm
    grad_branch = grad_resid.astype(jnp.bfloat16)
    hidden_again, grad_branch = lax.optimization_barrier((hidden, grad_branch))
    forward_parts = attention_forward(hidden_again)
    normed_all, queries, pairs_all, totals, summed, norm_back = forward_parts
    attention_back = summed.astype(jnp.bfloat16)
    branch_all = lax.all_gather(grad_branch, "tp", axis=0, tiled=True)
    grad_dense_w = inner_rows(attention_back, branch_all)
    grad_attention = times_transposed(branch_all, dense_w).astype(jnp.bfloat16)

    def backward_group(inputs):
        query_blk, pair_blk, lengths_blk, totals_blk, grad_blk = inputs
        masked = masked_scores(
            query_blk, pair_blk[:, :, 0], lengths_blk, slopes, distance, causal_mask, key_places
        )
        probabilities = jnp.exp(masked - totals_blk[..., None])
        grad_probs = jnp.einsum(
            "gihd,gjhd->ghij", grad_blk, pair_blk[:, :, 1], preferred_element_type=jnp.float32
        )
        row_delta = jnp.sum(probabilities * grad_probs, axis=-1, keepdims=True)
        grad_scores = (probabilities * (grad_probs - row_delta)).astype(jnp.bfloat16)
        grad_query = (
            jnp.einsum(
                "ghij,gjhd->gihd",
                grad_scores,
                pair_blk[:, :, 0],
                preferred_element_type=jnp.float32,
            )
            * 0.125
        )
        grad_key = (
            jnp.einsum(
                "ghij,gihd->gjhd", grad_scores, query_blk, preferred_element_type=jnp.float32
            )
            * 0.125
        )
        grad_value = jnp.einsum(
            "ghij,gihd->gjhd",
            probabilities.astype(jnp.bfloat16),
            grad_blk,
            preferred_element_type=jnp.float32,
        )
        return (grad_query, jnp.stack([grad_key, grad_value], axis=2))

    grad_query_all, grad_pairs = lax.map(
        backward_group,
        (
            query_view(queries),
            pair_view(pairs_all),
            grouped_lengths,
            totals,
            query_view(grad_attention),
        ),
    )
    grad_pairs_local = lax.psum_scatter(
        grad_pairs.reshape(slot_total, slot_len, 2 * head_width).astype(jnp.bfloat16),
        "wide",
        scatter_dimension=1,
        tiled=True,
    ).astype(jnp.float32)
    grad_queries = grad_query_all.reshape(slot_total, block_len, head_width).astype(jnp.bfloat16)
    grad_keys = grad_pairs_local[:, :, :head_width].astype(jnp.bfloat16)
    grad_values = grad_pairs_local[:, :, head_width:].astype(jnp.bfloat16)
    grad_query_w = inner_rows(normed_all, grad_queries)
    grad_key_w = inner_rows(normed_all, grad_keys)
    grad_value_w = inner_rows(normed_all, grad_values)
    grad_query_b = jnp.sum(flatten_rows(grad_queries), axis=0, dtype=jnp.float32).reshape(
        heads_dev, HEAD
    )
    grad_value_b = jnp.sum(flatten_rows(grad_values), axis=0, dtype=jnp.float32).reshape(
        heads_dev, HEAD
    )
    grad_normed = lax.psum_scatter(
        (
            times_transposed(grad_queries, query_w)
            + times_transposed(grad_keys, key_w)
            + times_transposed(grad_values, value_w)
        ).astype(jnp.bfloat16),
        "tp",
        scatter_dimension=0,
        tiled=True,
    ).astype(jnp.float32)
    grad_hidden_norm, grad_gain_one, grad_shift_one = norm_back(grad_normed)
    grad_in = (grad_resid + grad_hidden_norm).astype(jnp.bfloat16)
    (
        sum_query_w,
        sum_key_w,
        sum_value_w,
        sum_query_b,
        sum_value_b,
        sum_dense_w,
        sum_up_w,
        sum_up_b,
        sum_down_w,
    ) = (
        lax.psum_scatter(
            grad_query_w.astype(jnp.bfloat16), "wide", scatter_dimension=0, tiled=True
        ).astype(jnp.float32),
        lax.psum_scatter(
            grad_key_w.astype(jnp.bfloat16), "wide", scatter_dimension=0, tiled=True
        ).astype(jnp.float32),
        lax.psum_scatter(
            grad_value_w.astype(jnp.bfloat16), "wide", scatter_dimension=0, tiled=True
        ).astype(jnp.float32),
        lax.psum_scatter(
            grad_query_b.astype(jnp.bfloat16), "wide", scatter_dimension=1, tiled=True
        ).astype(jnp.float32),
        lax.psum_scatter(
            grad_value_b.astype(jnp.bfloat16), "wide", scatter_dimension=1, tiled=True
        ).astype(jnp.float32),
        lax.psum_scatter(
            grad_dense_w.astype(jnp.bfloat16), "wide", scatter_dimension=1, tiled=True
        ).astype(jnp.float32),
        lax.psum_scatter(
            grad_up.astype(jnp.bfloat16), "wide", scatter_dimension=0, tiled=True
        ).astype(jnp.float32),
        lax.psum_scatter(
            grad_up_b.astype(jnp.bfloat16), "wide", scatter_dimension=1, tiled=True
        ).astype(jnp.float32),
        lax.psum_scatter(
            grad_down_w.astype(jnp.bfloat16), "wide", scatter_dimension=1, tiled=True
        ).astype(jnp.float32),
    )
    grad_dense_b = jnp.sum(grad_resid, axis=(0, 1))
    grad_down_b = jnp.sum(grad_output, axis=(0, 1))
    sum_gain_one, sum_shift_one, sum_dense_b, sum_gain_two, sum_shift_two, sum_down_b = lax.psum(
        (grad_gain_one, grad_shift_one, grad_dense_b, grad_gain_two, grad_shift_two, grad_down_b),
        ("wide", "tp"),
    )

    def own_part(tensor):
        return lax.dynamic_slice_in_dim(tensor, wide_at * vec_part, vec_part, 0)

    return (
        output,
        grad_in,
        own_part(sum_gain_one),
        own_part(sum_shift_one),
        sum_query_w,
        sum_key_w,
        sum_value_w,
        sum_query_b,
        sum_value_b,
        sum_dense_w,
        own_part(sum_dense_b),
        own_part(sum_gain_two),
        own_part(sum_shift_two),
        sum_up_w,
        sum_up_b,
        sum_down_w,
        own_part(sum_down_b),
    )


def solution(mesh):
    return jax.shard_map(
        per_device,
        mesh=mesh,
        in_specs=(
            P("tp", "wide", None),
            P(),
            P("wide"),
            P("wide"),
            P("wide", "tp"),
            P("wide", "tp"),
            P("wide", "tp"),
            P("tp", "wide"),
            P("tp", "wide"),
            P("tp", "wide"),
            P("wide"),
            P("wide"),
            P("wide"),
            P("wide", "tp"),
            P("tp", "wide"),
            P("tp", "wide"),
            P("wide"),
            P("tp", "wide", None),
        ),
        out_specs=(
            P("tp", "wide", None),
            P("tp", "wide", None),
            P("wide"),
            P("wide"),
            P("wide", "tp"),
            P("wide", "tp"),
            P("wide", "tp"),
            P("tp", "wide"),
            P("tp", "wide"),
            P("tp", "wide"),
            P("wide"),
            P("wide"),
            P("wide"),
            P("wide", "tp"),
            P("tp", "wide"),
            P("tp", "wide"),
            P("wide"),
        ),
        check_vma=False,
    )
```

profile of v0, /device:TPU:0, one launch (start us, length us, event | category | flops | bytes accessed | tf_op | source)
XLA Modules:
  0.0 1197.6 jit_solution(1751168843750282210)
XLA Ops:
  58.1 19.0 %all-gather.19.cloned.1.call-done = bf16[8,128,1024]{2,1,0:T(8,128)(2,1)} async-done(((bf16[2,128,1024]{2,1,0:T(8,128)(2,1)}), bf16[8,128,1024]{2,1,0:T(8,128)(2,1)}) %all-gather.19.cloned.1.call-update) | async-done | bytes 2097168 | tf_op jit(solution)/shard_map/all_gather | solution.py:157
  117.0 21.2 %all-gather.21.cloned.1.call-done = bf16[8,1024,512]{2,1,0:T(8,128)(2,1)} async-done(((bf16[8,128,512]{2,1,0:T(8,128)(2,1)}), bf16[8,1024,512]{2,1,0:T(8,128)(2,1)}) %all-gather.21.cloned.1.call-update) | async-done | bytes 8388624 | tf_op jit(solution)/shard_map/all_gather | solution.py:166
  149.8 21.8 %while.40 = (s32[]{:T(128)}, bf16[2,4,128,4,64]{2,4,3,1,0:T(8,128)(2,1)S(1)}, bf16[2,4,1024,2,4,64]{2,5,4,3,1,0:T(8,128)(2,1)}, s32[2,4]{1,0:T(2,128)S(1)}, bf16...) while((s32[]{:T(128)}, ...), condition=%wide.region_5.6_spmd.clone.clone, body=%wide.region_2.5_spmd.clone.clone.sunk | while | flops 567674880 | bytes 50398400 | solution.py:167
  199.7 17.8 %reduce-scatter.21.cloned.1.call-done = bf16[2,128,1024]{2,1,0:T(8,128)(2,1)} async-done(((bf16[8,128,1024]{2,1,0:T(8,128)(2,1)}), bf16[2,128,1024]{2,1,0:T(8,128)(2,1)}) %reduce-scatter.21.cloned.1.call-update) | async-done | bytes 524304 | tf_op jit(solution)/shard_map/reduce_scatter | solution.py:181
  246.3 47.7 %all-gather.23.cloned.1.call-done = bf16[8,128,1024]{2,1,0:T(8,128)(2,1)} async-done(((bf16[2,128,1024]{2,1,0:T(8,128)(2,1)}), bf16[8,128,1024]{2,1,0:T(8,128)(2,1)}) %all-gather.23.cloned.1.call-update) | async-done | bytes 2097168 | tf_op jit(solution)/shard_map/all_gather | solution.py:190
  300.6 40.0 %all-gather.29.cloned.1.call-done = bf16[8,128,1024]{2,1,0:T(8,128)(2,1)} async-done(((bf16[2,128,1024]{2,1,0:T(8,128)(2,1)}), bf16[8,128,1024]{2,1,0:T(8,128)(2,1)}) %all-gather.29.cloned.1.call-update) | async-done | bytes 2097168 | tf_op jit(solution)/shard_map/all_gather | solution.py:191
  340.5 28.8 %all-gather.27.cloned.1.call-done = bf16[1024,1024]{1,0:T(8,128)(2,1)} async-done(((bf16[1024,128]{1,0:T(8,128)(2,1)}), bf16[1024,1024]{1,0:T(8,128)(2,1)}) %all-gather.27.cloned.1.call-update) | async-done | bytes 2097168 | tf_op jit(solution)/shard_map/all_gather | solution.py:115
  400.3 60.6 %reduce-scatter.25.cloned.1.call-done = f32[2,128,1024]{2,1,0:T(8,128)} async-done(((f32[8,128,1024]{2,1,0:T(8,128)}), f32[2,128,1024]{2,1,0:T(8,128)}) %reduce-scatter.25.cloned.1.call-update) | async-done | bytes 1048592 | tf_op jit(solution)/shard_map/reduce_scatter | solution.py:204
  463.2 44.1 %reduce-scatter.23.cloned.1.call-done = bf16[2,128,1024]{2,1,0:T(8,128)(2,1)} async-done(((bf16[8,128,1024]{2,1,0:T(8,128)(2,1)}), bf16[2,128,1024]{2,1,0:T(8,128)(2,1)}) %reduce-scatter.23.cloned.1.call-update) | async-done | bytes 524304 | tf_op jit(solution)/shard_map/reduce_scatter | solution.py:196
  514.5 44.2 %all-gather.31.cloned.1.call-done = bf16[8,128,1024]{2,1,0:T(8,128)(2,1)} async-done(((bf16[2,128,1024]{2,1,0:T(8,128)(2,1)}), bf16[8,128,1024]{2,1,0:T(8,128)(2,1)}) %all-gather.31.cloned.1.call-update) | async-done | bytes 2097168 | tf_op jit(solution)/shard_map/all_gather | solution.py:157
  564.6 40.7 %all-gather.35.cloned.1.call-done = bf16[8,128,1024]{2,1,0:T(8,128)(2,1)} async-done(((bf16[2,128,1024]{2,1,0:T(8,128)(2,1)}), bf16[8,128,1024]{2,1,0:T(8,128)(2,1)}) %all-gather.35.cloned.1.call-update) | async-done | bytes 2097168 | tf_op jit(solution)/shard_map/all_gather | solution.py:217
  610.6 49.6 %all-gather.33.cloned.1.call-done = bf16[8,1024,512]{2,1,0:T(8,128)(2,1)} async-done(((bf16[8,128,512]{2,1,0:T(8,128)(2,1)}), bf16[8,1024,512]{2,1,0:T(8,128)(2,1)}) %all-gather.33.cloned.1.call-update) | async-done | bytes 8388624 | tf_op jit(solution)/shard_map/all_gather | solution.py:166
  680.3 21.9 %while.41 = (s32[]{:T(128)}, f32[2,4,4,128]{3,2,1,0:T(4,128)S(1)}, bf16[2,4,128,4,64]{2,4,3,1,0:T(8,128)(2,1)S(1)}, s32[2,4]{1,0:T(2,128)S(1)}, bf16[2,4,128,4,6...) while((s32[]{:T(128)}, f32[2,4,4,128]{3,2,1,0:T(4,128)S(1)}, ...), condition=%wide.region_18.19_spmd.clone.clone, body=%wide.region_15.18_spmd.clone.clone.sunk | while | flops 567674880 | bytes 50406604 | solution.py:167
  703.1 35.1 %while.42 = (s32[]{:T(128)}, bf16[2,4,128,4,64]{2,4,3,1,0:T(8,128)(2,1)}, bf16[2,4,1024,2,4,64]{2,5,4,3,1,0:T(8,128)(2,1)}, bf16[2,4,1024,2,4,64]{2,5,4,1,3,0:T(...) while((s32[]{:T(128)}, ...), condition=%wide.region_21.22_spmd.clone.clone, body=%wide.region_19.21_spmd.clone.clone.sunk | while | flops 1368918016 | bytes 161269104 | solution.py:255
  773.6 47.6 %reduce-scatter.27.cloned.1.call-done = bf16[8,128,512]{2,1,0:T(8,128)(2,1)} async-done(((bf16[8,1024,512]{2,1,0:T(8,128)(2,1)}), bf16[8,128,512]{2,1,0:T(8,128)(2,1)}) %reduce-scatter.27.cloned.1.call-update) | async-done | bytes 1048592 | tf_op jit(solution)/shard_map/reduce_scatter | solution.py:265
  834.8 23.4 %reduce-scatter.41.cloned.1.call-done = bf16[32,4]{1,0:T(8,128)(2,1)} async-done(((bf16[256,4]{1,0:T(8,128)(2,1)}), bf16[32,4]{1,0:T(8,128)(2,1)}) %reduce-scatter.41.cloned.1.call-update) | async-done | bytes 272
  859.5 42.9 %reduce-scatter.43.cloned.1.call-done = bf16[128,1024]{1,0:T(8,128)(2,1)} async-done(((bf16[1024,1024]{1,0:T(8,128)(2,1)}), bf16[128,1024]{1,0:T(8,128)(2,1)}) %reduce-scatter.43.cloned.1.call-update) | async-done | bytes 262160
  904.4 42.3 %reduce-scatter.37.cloned.1.call-done = bf16[128,1024]{1,0:T(8,128)(2,1)} async-done(((bf16[1024,1024]{1,0:T(8,128)(2,1)}), bf16[128,1024]{1,0:T(8,128)(2,1)}) %reduce-scatter.37.cloned.1.call-update) | async-done | bytes 262160 | tf_op jit(solution)/shard_map/reduce_scatter | solution.py:324
  948.6 35.2 %reduce-scatter.39.cloned.1.call-done = bf16[128,256]{1,0:T(8,128)(2,1)} async-done(((bf16[1024,256]{1,0:T(8,128)(2,1)}), bf16[128,256]{1,0:T(8,128)(2,1)}) %reduce-scatter.39.cloned.1.call-update) | async-done | bytes 65552
  985.4 35.5 %reduce-scatter.31.cloned.1.call-done = bf16[128,256]{1,0:T(8,128)(2,1)} async-done(((bf16[1024,256]{1,0:T(8,128)(2,1)}), bf16[128,256]{1,0:T(8,128)(2,1)}) %reduce-scatter.31.cloned.1.call-update) | async-done | bytes 65552 | tf_op jit(solution)/shard_map/reduce_scatter | solution.py:306
  1036.5 21.7 %reduce-scatter.35.cloned.1.call-done = bf16[128,256]{1,0:T(8,128)(2,1)} async-done(((bf16[1024,256]{1,0:T(8,128)(2,1)}), bf16[128,256]{1,0:T(8,128)(2,1)}) %reduce-scatter.35.cloned.1.call-update) | async-done | bytes 65552 | tf_op jit(solution)/shard_map/reduce_scatter | solution.py:312
  1059.7 36.2 %reduce-scatter.33.cloned.1.call-done = bf16[128,256]{1,0:T(8,128)(2,1)} async-done(((bf16[1024,256]{1,0:T(8,128)(2,1)}), bf16[128,256]{1,0:T(8,128)(2,1)}) %reduce-scatter.33.cloned.1.call-update) | async-done | bytes 65552 | tf_op jit(solution)/shard_map/reduce_scatter | solution.py:309
  1097.4 44.5 %reduce-scatter.29.cloned.1.call-done = bf16[2,128,1024]{2,1,0:T(8,128)(2,1)} async-done(((bf16[8,128,1024]{2,1,0:T(8,128)(2,1)}), bf16[2,128,1024]{2,1,0:T(8,128)(2,1)}) %reduce-scatter.29.cloned.1.call-update) | async-done | bytes 524304 | tf_op jit(solution)/shard_map/reduce_scatter | solution.py:283
  1147.3 39.7 %all-reduce.2 = (f32[1024]{0:T(1024)S(1)}, f32[1024]{0:T(1024)S(1)}, f32[1024]{0:T(1024)S(1)}, f32[1024]{0:T(1024)S(1)}, f32[1024]{0:T(1024)S(1)}, /*index=5*/f32[1024]{0:T(1024)S(1)}) all-reduce(f32[1024]{0:T(1024)S(1)} %get-tuple-element.442, f32[1024]{0:T(1024)S(1)} %get-tuple-element.447, ...), channel_id=1, replica_groups=mesh['wide'=8,'tp'=4] {'wide','tp'}, use_global_device_ids=true, to_apply=%region_27.28 | all-reduce | flops 6144 | bytes 49152 | tf_op jit(solution)/shard_map/psum | solution.py:336
  (371 shorter events, 397.8 us)
Async XLA Ops:
  7.2 69.9 %all-gather.19.cloned.1.call-start = ((), (), s32[]{:S(2)}) async-start(), calls=%async_computation.12 | async-start | bytes 2621440 | tf_op jit(solution)/shard_map/all_gather | solution.py:157
  20.2 492.4 %copy-start.26 = (f32[8,1,128]{2,1,0:T(1,128)}, f32[8,1,128]{2,1,0:T(1,128)S(1)}, u32[]{:S(2)}) copy-start(f32[8,1,128]{2,1,0:T(1,128)S(1)} %convert_element_type.303) | copy-start | bytes 12292
  30.9 107.2 %all-gather.21.cloned.1.call-start = ((), (), s32[]{:S(2)}) async-start(), calls=%async_computation.13 | async-start | bytes 9437184 | tf_op jit(solution)/shard_map/all_gather | solution.py:166
  58.1 502.9 %copy-start.14 = (bf16[1024,256]{1,0:T(8,128)(2,1)}, bf16[1024,256]{1,0:T(8,128)(2,1)S(1)}, u32[]{:S(2)}) copy-start(bf16[1024,256]{1,0:T(8,128)(2,1)S(1)} %all_gather.70) | copy-start | bytes 1572868
  82.9 134.6 %reduce-scatter.21.cloned.1.call-start = ((), (), s32[]{:S(2)}) async-start(), calls=%async_computation.14 | async-start | bytes 2621440 | tf_op jit(solution)/shard_map/reduce_scatter | solution.py:181
  173.7 72.6 %all-gather.25.cloned.1.call-start = ((), (), s32[]{:S(2)}) async-start(), calls=%async_computation.16 | async-start | bytes 2359296 | tf_op jit(solution)/shard_map/all_gather | solution.py:113
  174.3 119.7 %all-gather.23.cloned.1.call-start = ((), (), s32[]{:S(2)}) async-start(), calls=%async_computation.15 | async-start | bytes 2621440 | tf_op jit(solution)/shard_map/all_gather | solution.py:190
  222.4 118.1 %all-gather.29.cloned.1.call-start = ((), (), s32[]{:S(2)}) async-start(), calls=%async_computation.19 | async-start | bytes 2621440 | tf_op jit(solution)/shard_map/all_gather | solution.py:191
  223.6 145.8 %all-gather.27.cloned.1.call-start = ((), (), s32[]{:S(2)}) async-start(), calls=%async_computation.17 | async-start | bytes 2359296 | tf_op jit(solution)/shard_map/all_gather | solution.py:115
  224.3 236.6 %reduce-scatter.25.cloned.1.call-start = ((), (), s32[]{:S(2)}) async-start(), calls=%async_computation.20 | async-start | bytes 5242880 | tf_op jit(solution)/shard_map/reduce_scatter | solution.py:204
  384.0 123.4 %reduce-scatter.23.cloned.1.call-start = ((), (), s32[]{:S(2)}) async-start(), calls=%async_computation.18 | async-start | bytes 2621440 | tf_op jit(solution)/shard_map/reduce_scatter | solution.py:196
  391.1 167.6 %all-gather.31.cloned.1.call-start = ((), (), s32[]{:S(2)}) async-start(), calls=%async_computation.21 | async-start | bytes 2621440 | tf_op jit(solution)/shard_map/all_gather | solution.py:157
  513.7 91.7 %all-gather.35.cloned.1.call-start = ((), (), s32[]{:S(2)}) async-start(), calls=%async_computation.23 | async-start | bytes 2621440 | tf_op jit(solution)/shard_map/all_gather | solution.py:217
  514.4 145.8 %all-gather.33.cloned.1.call-start = ((), (), s32[]{:S(2)}) async-start(), calls=%async_computation.22 | async-start | bytes 9437184 | tf_op jit(solution)/shard_map/all_gather | solution.py:166
  564.6 256.6 %reduce-scatter.27.cloned.1.call-start = ((), (), s32[]{:S(2)}) async-start(), calls=%async_computation.24 | async-start | bytes 9437184 | tf_op jit(solution)/shard_map/reduce_scatter | solution.py:265
  749.6 108.5 %reduce-scatter.41.cloned.1.call-start = ((), (), s32[]{:S(2)}) async-start(), calls=%async_computation.31 | async-start | bytes 73728
  751.1 151.3 %reduce-scatter.43.cloned.1.call-start = ((), (), s32[]{:S(2)}) async-start(), calls=%async_computation.32 | async-start | bytes 2359296
  759.9 186.7 %reduce-scatter.37.cloned.1.call-start = ((), (), s32[]{:S(2)}) async-start(), calls=%async_computation.29 | async-start | bytes 2359296 | tf_op jit(solution)/shard_map/reduce_scatter | solution.py:324
  766.8 217.0 %reduce-scatter.39.cloned.1.call-start = ((), (), s32[]{:S(2)}) async-start(), calls=%async_computation.30 | async-start | bytes 589824
  770.3 250.6 %reduce-scatter.31.cloned.1.call-start = ((), (), s32[]{:S(2)}) async-start(), calls=%async_computation.26 | async-start | bytes 589824 | tf_op jit(solution)/shard_map/reduce_scatter | solution.py:306
  773.5 284.6 %reduce-scatter.35.cloned.1.call-start = ((), (), s32[]{:S(2)}) async-start(), calls=%async_computation.28 | async-start | bytes 589824 | tf_op jit(solution)/shard_map/reduce_scatter | solution.py:312
  824.4 271.4 %reduce-scatter.33.cloned.1.call-start = ((), (), s32[]{:S(2)}) async-start(), calls=%async_computation.27 | async-start | bytes 589824 | tf_op jit(solution)/shard_map/reduce_scatter | solution.py:309
  828.8 313.0 %reduce-scatter.29.cloned.1.call-start = ((), (), s32[]{:S(2)}) async-start(), calls=%async_computation.25 | async-start | bytes 2621440 | tf_op jit(solution)/shard_map/reduce_scatter | solution.py:283
  833.3 311.5 %copy-start.6 = (f32[2,128,1024]{2,1,0:T(8,128)S(1)}, f32[2,128,1024]{2,1,0:T(8,128)}, u32[]{:S(2)}) copy-start(f32[2,128,1024]{2,1,0:T(8,128)} %copy-done.5) | copy-start | bytes 3145732
  (60 other events, 4252.9 us)
Sparse Core Ops, SparseCore 0:
  31.1 45.9 all-gather.18
  83.0 55.0 all-gather.20
  173.9 43.6 reduce-scatter.20
  219.3 27.0 all-gather.24
  248.3 45.6 all-gather.22
  296.0 44.4 all-gather.28
  342.4 26.8 all-gather.26
  384.1 76.7 reduce-scatter.24
  463.2 44.0 reduce-scatter.22
  513.8 44.8 all-gather.30
  560.9 44.4 all-gather.34
  607.1 53.0 all-gather.32
  749.8 71.3 reduce-scatter.26
  824.6 33.5 reduce-scatter.40
  861.3 41.0 reduce-scatter.42
  905.6 41.0 reduce-scatter.36
  949.6 34.1 reduce-scatter.38
  986.7 34.1 reduce-scatter.30
  1024.0 34.1 reduce-scatter.34
  1061.7 34.1 reduce-scatter.32
  1098.2 43.6 reduce-scatter.28
where the time goes:
time: 1200 us
  waiting for transfers between devices  758 us (63%)
  blocking collectives  172 us (14%)
  matrix products  108 us (9%)
  local copies, waits for them, and re-layouts  86.3 us (7%)
  other arithmetic  54.7 us (5%)
  between operations  16.1 us (1%)
    unnamed x24, waiting for transfers between devices  104 us
    all_gather x2, waiting for transfers between devices, attention_forward(): pairs_all = lax.all_gather(pairs, 'wide', axis=1, tiled=True)  70.8 us
    all_gather x2, waiting for transfers between devices, attention_forward(): normed_all = lax.all_gather(normed, 'tp', axis=0, tiled=True)  63.2 us
    reduce_scatter x1, waiting for transfers between devices, per_device(): lax.psum_scatter(times_transposed(grad_pre, up_w), 'tp', scatter_dimensio...  60.6 us
    all_gather x1, waiting for transfers between devices, per_device(): lax.all_gather(second, 'tp', axis=0, tiled=True)  47.7 us
    reduce_scatter x1, waiting for transfers between devices, per_device(): lax.psum_scatter(grad_pairs.reshape(slot_total, slot_len, 2 * head_width)...  47.6 us
    reduce_scatter x1, waiting for transfers between devices, per_device(): lax.psum_scatter((times_transposed(grad_queries, query_w) + times_transpo...  44.5 us
    reduce_scatter x1, waiting for transfers between devices, per_device(): lax.psum_scatter(row_product(activated, down_w).astype(jnp.bfloat16), 'tp...  44.1 us
  transfers between devices with their start and end apart: 21, of which 21 were waited for; matrix products, arithmetic and copies ran while one was open for 7% of the time, Pallas kernels for 0%

commit v1 on v0

--- a/solution.py
+++ b/solution.py
@@ -5,6 +5,19 @@
 from jax.sharding import PartitionSpec as P
 
 HEAD = 64
+
+
+def collect(array, axis, dim):
+    count, index, rows = (lax.axis_size(axis), lax.axis_index(axis), array.shape[dim])
+    forward = [(i, (i + 1) % count) for i in range(count)]
+    out = jnp.zeros((*array.shape[:dim], count * rows, *array.shape[dim + 1 :]), array.dtype)
+    held = array
+    for step in range(count):
+        owner = (index - step) % count
+        out = lax.dynamic_update_slice_in_dim(out, held, owner * rows, axis=dim)
+        if step < count - 1:
+            held = lax.ppermute(held, axis, forward)
+    return out
 
 
 def norm_rows(values, gain_vec, shift_vec):
@@ -112,7 +125,7 @@
         lax.all_gather(mid_shift, "wide", axis=0, tiled=True),
         lax.all_gather(w_up, "wide", axis=0, tiled=True),
         lax.all_gather(b_up, "wide", axis=1, tiled=True),
-        lax.all_gather(w_down, "wide", axis=1, tiled=True),
+        collect(w_down, "wide", 1),
         lax.all_gather(b_down, "wide", axis=0, tiled=True),
     )
     gain_one = gain_one.astype(jnp.float32)

time: 1200 us -> 1180 us (0.983)
  waiting for transfers between devices: 758 us -> 722 us
    ppermute x0 -> x7, waiting for transfers between devices: none -> 37.4 us  [collect(): held = lax.ppermute(held, axis, forward)]
    all_gather x1, waiting for transfers between devices: 47.7 us -> 17.7 us  [per_device(): lax.all_gather(second, 'tp', axis=0, tiled=True)]
    all_gather x1 -> x0, waiting for transfers between devices: 28.8 us -> none  [per_device(): lax.all_gather(w_down, 'wide', axis=1, tiled=True)]
    all_gather x1, waiting for transfers between devices: 12.8 us -> 0.01 us  [per_device(): lax.all_gather(w_up, 'wide', axis=0, tiled=True)]
    unnamed x24 -> x23, waiting for transfers between devices: 104 us -> 103 us
  transfers between devices with their start and end apart: 21 -> 27, of which waited for: 21 -> 25; matrix products, arithmetic and copies ran while one was open for 7% -> 8% of each run, Pallas kernels for 0% -> 0%
where the time goes in v1:
time: 1180 us; the launch traced here: 1170 us
  waiting for transfers between devices  722 us (61%)
  blocking collectives  172 us (15%)
  matrix products  109 us (9%)
  local copies, waits for them, and re-layouts  94.2 us (8%)
  other arithmetic  54.7 us (5%)
  between operations  16.1 us (1%)
    unnamed x23, waiting for transfers between devices  103 us
    all_gather x2, waiting for transfers between devices, attention_forward(): pairs_all = lax.all_gather(pairs, 'wide', axis=1, tiled=True)  71 us
    all_gather x2, waiting for transfers between devices, attention_forward(): normed_all = lax.all_gather(normed, 'tp', axis=0, tiled=True)  63.3 us
    reduce_scatter x1, waiting for transfers between devices, per_device(): lax.psum_scatter(times_transposed(grad_pre, up_w), 'tp', scatter_dimensio...  59.4 us
    reduce_scatter x1, waiting for transfers between devices, per_device(): lax.psum_scatter(grad_pairs.reshape(slot_total, slot_len, 2 * head_width)...  47.5 us
    reduce_scatter x1, waiting for transfers between devices, per_device(): lax.psum_scatter((times_transposed(grad_queries, query_w) + times_transpo...  44.3 us
    reduce_scatter x1, waiting for transfers between devices, per_device(): lax.psum_scatter(row_product(activated, down_w).astype(jnp.bfloat16), 'tp...  44.1 us
    reduce_scatter x1, waiting for transfers between devices, per_device(): lax.psum_scatter(grad_up.astype(jnp.bfloat16), 'wide', scatter_dimension=...  42.3 us
  transfers between devices with their start and end apart: 27, of which 25 were waited for; matrix products, arithmetic and copies ran while one was open for 8% of the time, Pallas kernels for 0%

profile of v1, /device:TPU:0, one launch (start us, length us, event | category | flops | bytes accessed | tf_op | source)
XLA Modules:
  0.0 1169.6 jit_solution(1851547322106823449)
XLA Ops:
  58.1 19.0 %all-gather.18.cloned.1.call-done = bf16[8,128,1024]{2,1,0:T(8,128)(2,1)} async-done(((bf16[2,128,1024]{2,1,0:T(8,128)(2,1)}), bf16[8,128,1024]{2,1,0:T(8,128)(2,1)}) %all-gather.18.cloned.1.call-update) | async-done | bytes 2097168 | tf_op jit(solution)/shard_map/all_gather | solution.py:170
  92.0 12.5 %all_gather.70 = bf16[1024,256]{1,0:T(8,128)(2,1)S(1)} all-gather(bf16[128,256]{1,0:T(8,128)(2,1)S(1)} %copy-done.29), channel_id=1, replica_groups=mesh['wide'=8,'tp'=4] {'wide'}, dimensions={0}, use_global_device_ids=true | all-gather | bytes 589824 | tf_op jit(solution)/shard_map/all_gather | solution.py:117
  117.0 21.2 %all-gather.20.cloned.1.call-done = bf16[8,1024,512]{2,1,0:T(8,128)(2,1)} async-done(((bf16[8,128,512]{2,1,0:T(8,128)(2,1)}), bf16[8,1024,512]{2,1,0:T(8,128)(2,1)}) %all-gather.20.cloned.1.call-update) | async-done | bytes 8388624 | tf_op jit(solution)/shard_map/all_gather | solution.py:179
  149.8 21.8 %while.40 = (s32[]{:T(128)}, bf16[2,4,128,4,64]{2,4,3,1,0:T(8,128)(2,1)S(1)}, bf16[2,4,1024,2,4,64]{2,5,4,3,1,0:T(8,128)(2,1)}, s32[2,4]{1,0:T(2,128)S(1)}, bf16...) while((s32[]{:T(128)}, ...), condition=%wide.region_5.6_spmd.clone.clone, body=%wide.region_2.5_spmd.clone.clone.sunk | while | flops 567674880 | bytes 50398400 | solution.py:180
  199.7 17.8 %reduce-scatter.21.cloned.1.call-done = bf16[2,128,1024]{2,1,0:T(8,128)(2,1)} async-done(((bf16[8,128,1024]{2,1,0:T(8,128)(2,1)}), bf16[2,128,1024]{2,1,0:T(8,128)(2,1)}) %reduce-scatter.21.cloned.1.call-update) | async-done | bytes 524304 | tf_op jit(solution)/shard_map/reduce_scatter | solution.py:194
  278.4 17.7 %all-gather.22.cloned.1.call-done = bf16[8,128,1024]{2,1,0:T(8,128)(2,1)} async-done(((bf16[2,128,1024]{2,1,0:T(8,128)(2,1)}), bf16[8,128,1024]{2,1,0:T(8,128)(2,1)}) %all-gather.22.cloned.1.call-update) | async-done | bytes 2097168 | tf_op jit(solution)/shard_map/all_gather | solution.py:203
  302.7 39.9 %all-gather.26.cloned.1.call-done = bf16[8,128,1024]{2,1,0:T(8,128)(2,1)} async-done(((bf16[2,128,1024]{2,1,0:T(8,128)(2,1)}), bf16[8,128,1024]{2,1,0:T(8,128)(2,1)}) %all-gather.26.cloned.1.call-update) | async-done | bytes 2097168 | tf_op jit(solution)/shard_map/all_gather | solution.py:204
  373.5 59.4 %reduce-scatter.25.cloned.1.call-done = f32[2,128,1024]{2,1,0:T(8,128)} async-done(((f32[8,128,1024]{2,1,0:T(8,128)}), f32[2,128,1024]{2,1,0:T(8,128)}) %reduce-scatter.25.cloned.1.call-update) | async-done | bytes 1048592 | tf_op jit(solution)/shard_map/reduce_scatter | solution.py:217
  435.3 44.1 %reduce-scatter.23.cloned.1.call-done = bf16[2,128,1024]{2,1,0:T(8,128)(2,1)} async-done(((bf16[8,128,1024]{2,1,0:T(8,128)(2,1)}), bf16[2,128,1024]{2,1,0:T(8,128)(2,1)}) %reduce-scatter.23.cloned.1.call-update) | async-done | bytes 524304 | tf_op jit(solution)/shard_map/reduce_scatter | solution.py:209
  486.5 44.4 %all-gather.28.cloned.1.call-done = bf16[8,128,1024]{2,1,0:T(8,128)(2,1)} async-done(((bf16[2,128,1024]{2,1,0:T(8,128)(2,1)}), bf16[8,128,1024]{2,1,0:T(8,128)(2,1)}) %all-gather.28.cloned.1.call-update) | async-done | bytes 2097168 | tf_op jit(solution)/shard_map/all_gather | solution.py:170
  536.7 40.6 %all-gather.32.cloned.1.call-done = bf16[8,128,1024]{2,1,0:T(8,128)(2,1)} async-done(((bf16[2,128,1024]{2,1,0:T(8,128)(2,1)}), bf16[8,128,1024]{2,1,0:T(8,128)(2,1)}) %all-gather.32.cloned.1.call-update) | async-done | bytes 2097168 | tf_op jit(solution)/shard_map/all_gather | solution.py:230
  582.5 49.8 %all-gather.30.cloned.1.call-done = bf16[8,1024,512]{2,1,0:T(8,128)(2,1)} async-done(((bf16[8,128,512]{2,1,0:T(8,128)(2,1)}), bf16[8,1024,512]{2,1,0:T(8,128)(2,1)}) %all-gather.30.cloned.1.call-update) | async-done | bytes 8388624 | tf_op jit(solution)/shard_map/all_gather | solution.py:179
  652.4 21.9 %while.41 = (s32[]{:T(128)}, f32[2,4,4,128]{3,2,1,0:T(4,128)S(1)}, bf16[2,4,128,4,64]{2,4,3,1,0:T(8,128)(2,1)S(1)}, s32[2,4]{1,0:T(2,128)S(1)}, bf16[2,4,128,4,6...) while((s32[]{:T(128)}, f32[2,4,4,128]{3,2,1,0:T(4,128)S(1)}, ...), condition=%wide.region_18.19_spmd.clone.clone, body=%wide.region_15.18_spmd.clone.clone.sunk | while | flops 567674880 | bytes 50406604 | solution.py:180
  675.2 35.0 %while.42 = (s32[]{:T(128)}, bf16[2,4,128,4,64]{2,4,3,1,0:T(8,128)(2,1)}, bf16[2,4,1024,2,4,64]{2,5,4,3,1,0:T(8,128)(2,1)}, bf16[2,4,1024,2,4,64]{2,5,4,1,3,0:T(...) while((s32[]{:T(128)}, ...), condition=%wide.region_21.22_spmd.clone.clone, body=%wide.region_19.21_spmd.clone.clone.sunk | while | flops 1368918016 | bytes 161269104 | solution.py:268
  745.8 47.5 %reduce-scatter.27.cloned.1.call-done = bf16[8,128,512]{2,1,0:T(8,128)(2,1)} async-done(((bf16[8,1024,512]{2,1,0:T(8,128)(2,1)}), bf16[8,128,512]{2,1,0:T(8,128)(2,1)}) %reduce-scatter.27.cloned.1.call-update) | async-done | bytes 1048592 | tf_op jit(solution)/shard_map/reduce_scatter | solution.py:278
  806.9 23.5 %reduce-scatter.41.cloned.1.call-done = bf16[32,4]{1,0:T(8,128)(2,1)} async-done(((bf16[256,4]{1,0:T(8,128)(2,1)}), bf16[32,4]{1,0:T(8,128)(2,1)}) %reduce-scatter.41.cloned.1.call-update) | async-done | bytes 272
  831.8 42.9 %reduce-scatter.43.cloned.1.call-done = bf16[128,1024]{1,0:T(8,128)(2,1)} async-done(((bf16[1024,1024]{1,0:T(8,128)(2,1)}), bf16[128,1024]{1,0:T(8,128)(2,1)}) %reduce-scatter.43.cloned.1.call-update) | async-done | bytes 262160
  876.6 42.3 %reduce-scatter.37.cloned.1.call-done = bf16[128,1024]{1,0:T(8,128)(2,1)} async-done(((bf16[1024,1024]{1,0:T(8,128)(2,1)}), bf16[128,1024]{1,0:T(8,128)(2,1)}) %reduce-scatter.37.cloned.1.call-update) | async-done | bytes 262160 | tf_op jit(solution)/shard_map/reduce_scatter | solution.py:337
  920.9 35.1 %reduce-scatter.39.cloned.1.call-done = bf16[128,256]{1,0:T(8,128)(2,1)} async-done(((bf16[1024,256]{1,0:T(8,128)(2,1)}), bf16[128,256]{1,0:T(8,128)(2,1)}) %reduce-scatter.39.cloned.1.call-update) | async-done | bytes 65552
  957.7 35.5 %reduce-scatter.31.cloned.1.call-done = bf16[128,256]{1,0:T(8,128)(2,1)} async-done(((bf16[1024,256]{1,0:T(8,128)(2,1)}), bf16[128,256]{1,0:T(8,128)(2,1)}) %reduce-scatter.31.cloned.1.call-update) | async-done | bytes 65552 | tf_op jit(solution)/shard_map/reduce_scatter | solution.py:319
  1008.7 21.5 %reduce-scatter.35.cloned.1.call-done = bf16[128,256]{1,0:T(8,128)(2,1)} async-done(((bf16[1024,256]{1,0:T(8,128)(2,1)}), bf16[128,256]{1,0:T(8,128)(2,1)}) %reduce-scatter.35.cloned.1.call-update) | async-done | bytes 65552 | tf_op jit(solution)/shard_map/reduce_scatter | solution.py:325
  1031.7 36.3 %reduce-scatter.33.cloned.1.call-done = bf16[128,256]{1,0:T(8,128)(2,1)} async-done(((bf16[1024,256]{1,0:T(8,128)(2,1)}), bf16[128,256]{1,0:T(8,128)(2,1)}) %reduce-scatter.33.cloned.1.call-update) | async-done | bytes 65552 | tf_op jit(solution)/shard_map/reduce_scatter | solution.py:322
  1069.5 44.3 %reduce-scatter.29.cloned.1.call-done = bf16[2,128,1024]{2,1,0:T(8,128)(2,1)} async-done(((bf16[8,128,1024]{2,1,0:T(8,128)(2,1)}), bf16[2,128,1024]{2,1,0:T(8,128)(2,1)}) %reduce-scatter.29.cloned.1.call-update) | async-done | bytes 524304 | tf_op jit(solution)/shard_map/reduce_scatter | solution.py:296
  1119.4 39.7 %all-reduce.2 = (f32[1024]{0:T(1024)S(1)}, f32[1024]{0:T(1024)S(1)}, f32[1024]{0:T(1024)S(1)}, f32[1024]{0:T(1024)S(1)}, f32[1024]{0:T(1024)S(1)}, /*index=5*/f32[1024]{0:T(1024)S(1)}) all-reduce(f32[1024]{0:T(1024)S(1)} %get-tuple-element.442, f32[1024]{0:T(1024)S(1)} %get-tuple-element.447, ...), channel_id=1, replica_groups=mesh['wide'=8,'tp'=4] {'wide','tp'}, use_global_device_ids=true, to_apply=%region_27.28 | all-reduce | flops 6144 | bytes 49152 | tf_op jit(solution)/shard_map/psum | solution.py:349
  (393 shorter events, 417.4 us)
Async XLA Ops:
  7.2 69.9 %all-gather.18.cloned.1.call-start = ((), (), s32[]{:S(2)}) async-start(), calls=%async_computation.12 | async-start | bytes 2621440 | tf_op jit(solution)/shard_map/all_gather | solution.py:170
  30.9 107.2 %all-gather.20.cloned.1.call-start = ((), (), s32[]{:S(2)}) async-start(), calls=%async_computation.13 | async-start | bytes 9437184 | tf_op jit(solution)/shard_map/all_gather | solution.py:179
  82.9 134.7 %reduce-scatter.21.cloned.1.call-start = ((), (), s32[]{:S(2)}) async-start(), calls=%async_computation.14 | async-start | bytes 2621440 | tf_op jit(solution)/shard_map/reduce_scatter | solution.py:194
  173.8 104.7 %all-gather.24.cloned.1.call-start = ((), (), s32[]{:S(2)}) async-start(), calls=%async_computation.16 | async-start | bytes 2359296 | tf_op jit(solution)/shard_map/all_gather | solution.py:126
  174.4 121.8 %all-gather.22.cloned.1.call-start = ((), (), s32[]{:S(2)}) async-start(), calls=%async_computation.15 | async-start | bytes 2621440 | tf_op jit(solution)/shard_map/all_gather | solution.py:203
  222.4 120.2 %all-gather.26.cloned.1.call-start = ((), (), s32[]{:S(2)}) async-start(), calls=%async_computation.18 | async-start | bytes 2621440 | tf_op jit(solution)/shard_map/all_gather | solution.py:204
  223.6 209.4 %reduce-scatter.25.cloned.1.call-start = ((), (), s32[]{:S(2)}) async-start(), calls=%async_computation.19 | async-start | bytes 5242880 | tf_op jit(solution)/shard_map/reduce_scatter | solution.py:217
  223.7 8.4 collective-permute-start
  238.8 9.7 collective-permute-start.2
  248.5 9.0 collective-permute-start.3
  270.8 6.8 collective-permute-start.6
  357.2 122.2 %reduce-scatter.23.cloned.1.call-start = ((), (), s32[]{:S(2)}) async-start(), calls=%async_computation.17 | async-start | bytes 2621440 | tf_op jit(solution)/shard_map/reduce_scatter | solution.py:209
  364.4 166.4 %all-gather.28.cloned.1.call-start = ((), (), s32[]{:S(2)}) async-start(), calls=%async_computation.20 | async-start | bytes 2621440 | tf_op jit(solution)/shard_map/all_gather | solution.py:170
  485.8 91.5 %all-gather.32.cloned.1.call-start = ((), (), s32[]{:S(2)}) async-start(), calls=%async_computation.22 | async-start | bytes 2621440 | tf_op jit(solution)/shard_map/all_gather | solution.py:230
  486.4 145.9 %all-gather.30.cloned.1.call-start = ((), (), s32[]{:S(2)}) async-start(), calls=%async_computation.21 | async-start | bytes 9437184 | tf_op jit(solution)/shard_map/all_gather | solution.py:179
  536.7 256.7 %reduce-scatter.27.cloned.1.call-start = ((), (), s32[]{:S(2)}) async-start(), calls=%async_computation.23 | async-start | bytes 9437184 | tf_op jit(solution)/shard_map/reduce_scatter | solution.py:278
  721.8 108.7 %reduce-scatter.41.cloned.1.call-start = ((), (), s32[]{:S(2)}) async-start(), calls=%async_computation.30 | async-start | bytes 73728
  723.2 151.5 %reduce-scatter.43.cloned.1.call-start = ((), (), s32[]{:S(2)}) async-start(), calls=%async_computation.31 | async-start | bytes 2359296
  732.1 186.9 %reduce-scatter.37.cloned.1.call-start = ((), (), s32[]{:S(2)}) async-start(), calls=%async_computation.28 | async-start | bytes 2359296 | tf_op jit(solution)/shard_map/reduce_scatter | solution.py:337
  739.0 217.1 %reduce-scatter.39.cloned.1.call-start = ((), (), s32[]{:S(2)}) async-start(), calls=%async_computation.29 | async-start | bytes 589824
  742.5 250.7 %reduce-scatter.31.cloned.1.call-start = ((), (), s32[]{:S(2)}) async-start(), calls=%async_computation.25 | async-start | bytes 589824 | tf_op jit(solution)/shard_map/reduce_scatter | solution.py:319
  745.7 284.5 %reduce-scatter.35.cloned.1.call-start = ((), (), s32[]{:S(2)}) async-start(), calls=%async_computation.27 | async-start | bytes 589824 | tf_op jit(solution)/shard_map/reduce_scatter | solution.py:325
  796.6 271.5 %reduce-scatter.33.cloned.1.call-start = ((), (), s32[]{:S(2)}) async-start(), calls=%async_computation.26 | async-start | bytes 589824 | tf_op jit(solution)/shard_map/reduce_scatter | solution.py:322
  800.9 312.9 %reduce-scatter.29.cloned.1.call-start = ((), (), s32[]{:S(2)}) async-start(), calls=%async_computation.24 | async-start | bytes 2621440 | tf_op jit(solution)/shard_map/reduce_scatter | solution.py:296
  (67 other events, 5517.2 us)
Sparse Core Ops, SparseCore 0:
  31.1 45.9 all-gather.17
  83.0 55.0 all-gather.19
  173.9 43.6 reduce-scatter.20
  219.3 27.9 all-gather.23
  249.3 46.7 all-gather.21
  298.1 44.4 all-gather.25
  357.3 75.5 reduce-scatter.24
  435.3 44.1 reduce-scatter.22
  485.9 44.8 all-gather.27
  532.8 44.4 all-gather.31
  579.2 53.0 all-gather.29
  721.9 71.3 reduce-scatter.26
  796.9 33.5 reduce-scatter.40
  833.6 41.0 reduce-scatter.42
  877.8 41.0 reduce-scatter.36
  921.9 34.1 reduce-scatter.38
  959.0 34.1 reduce-scatter.30
  996.1 34.1 reduce-scatter.34
  1033.9 34.1 reduce-scatter.32
  1070.2 43.6 reduce-scatter.28
